TPU v7x, 32 devices: a whole 2x2x4 slice. The times are simulated.
32 devices in a mesh: seq: 8 (over z, x), ch: 4 (over y, core).
Axes of the slice: x: 2, y: 2, z: 4, core: 2. Of those that a mesh axis runs over, the one named last changes fastest.
Arguments:
- block_input: bfloat16 [131072, 2048], P('seq', 'ch'), may hold values from -6 to 6
- gate_pre: bfloat16 [131072, 2048], P('seq', 'ch'), may hold values from -8 to 8
- out_grad: bfloat16 [131072, 2048], P('seq', 'ch'), may hold values from -6 to 6
- block_weight: bfloat16 [256, 512, 512], P('seq', 'ch'), may hold values from -0.25 to 0.25
- offset_weight: bfloat16 [512, 256, 256], P(('seq', 'ch')), may hold values from -0.375 to 0.375
- out_weight: bfloat16 [2048, 2048], P(None, 'ch'), may hold values from -0.125 to 0.125
- reset_offset: int32 [256], replicated, may hold values from 0 to 512, as said below
Outputs:
- input_grad: bfloat16 [131072, 2048], P('seq', 'ch')
- gate_grad: bfloat16 [131072, 2048], P('seq', 'ch')
- block_grad: bfloat16 [256, 512, 512], P('seq', 'ch')
- offset_grad: bfloat16 [512, 256, 256], P(('seq', 'ch'))
- out_weight_grad: bfloat16 [2048, 2048], P('seq', 'ch')
Inputs may be any that keep to these rules, and one draw needn't show every extreme that they name: reset_offset[0] is 0 and the last block starts no document; other blocks start a document at some place or none.
All inputs are finite; a program needn't handle non-finite values.
Results may differ from a plain program's by a relative error of at most 0.013.
Values may be sent and summed in bfloat16 or wider, within the bound.
No kernel may reach another device: no remote copies, remote signals or barrier semaphores. Data moves between devices by JAX's collectives and lax.ppermute only.
A program may use at most 512 MiB of HBM per device.

v0:
```python
import jax
import jax.numpy as jnp
from jax import lax
from jax.sharding import PartitionSpec as P


def side_flags_of(reset_offset, block_span):
    within = jnp.arange(block_span, dtype=jnp.int32)
    return within[None, :] >= reset_offset[:, None]


def document_ids(reset_offset, block_span):
    starts = (reset_offset < block_span).astype(jnp.int32)
    earlier = jnp.cumsum(starts) - starts
    return earlier[:, None] + side_flags_of(reset_offset, block_span).astype(jnp.int32)


def to_offsets(blocked, seq_count, ch_count):
    block_count, block_span, channels = blocked.shape
    arrived = lax.all_to_all(
        blocked.reshape(1, block_count, block_span, channels),
        ("seq", "ch"),
        split_axis=2,
        concat_axis=0,
        tiled=True,
    )
    return arrived.reshape(
        seq_count, ch_count, block_count, block_span // (seq_count * ch_count), channels
    )


def to_blocks(spread, seq_count, ch_count):
    block_count = spread.shape[2]
    offsets = spread.shape[3]
    channels = spread.shape[4]
    arrived = lax.all_to_all(
        spread.reshape(seq_count * ch_count, block_count, offsets, channels),
        ("seq", "ch"),
        split_axis=0,
        concat_axis=2,
        tiled=True,
    )
    return arrived.reshape(block_count, offsets * seq_count * ch_count, channels)


def on_device(
    block_input, gate_pre, out_grad, block_weight, offset_weight, out_weight, reset_offset
):
    seq_count = lax.axis_size("seq")
    ch_count = lax.axis_size("ch")
    token_count, channels = block_input.shape
    block_span = block_weight.shape[2]
    block_count = token_count // block_span
    offsets = block_span // (seq_count * ch_count)
    full_grad, full_weight = (
        lax.all_gather(out_grad, "ch", axis=1, tiled=True),
        lax.all_gather(block_weight, "ch", axis=1, tiled=True),
    )
    seq_index = lax.axis_index("seq")
    flat_index = seq_index * ch_count + lax.axis_index("ch")
    side_table = side_flags_of(reset_offset, block_span)
    doc_table = document_ids(reset_offset, block_span)
    total_blocks = doc_table.shape[0]
    local_sides = lax.dynamic_slice_in_dim(side_table, seq_index * block_count, block_count, 0)
    mask_one = local_sides[:, :, None] == local_sides[:, None, :]
    masked_one = jnp.where(mask_one, full_weight, jnp.zeros_like(full_weight))
    inputs = block_input.reshape(block_count, block_span, channels)
    section_out = jnp.einsum(
        "ikj,ijd->ikd", masked_one, inputs, preferred_element_type=jnp.float32
    ).astype(jnp.bfloat16)
    section_spread = to_offsets(section_out, seq_count, ch_count)
    labels = lax.dynamic_slice_in_dim(doc_table, flat_index * offsets, offsets, 1).T
    mask_two = labels[:, :, None] == labels[:, None, :]
    masked_two = jnp.where(mask_two, offset_weight, jnp.zeros_like(offset_weight))
    masked_two = masked_two.reshape(offsets, seq_count, block_count, seq_count, block_count)
    mixer_spread = jnp.einsum(
        "kpqsi,scikd->pcqkd", masked_two, section_spread, preferred_element_type=jnp.float32
    ).astype(jnp.bfloat16)
    mixer_out = to_blocks(mixer_spread, seq_count, ch_count).reshape(token_count, channels)
    head_grad = jnp.dot(full_grad, out_weight, preferred_element_type=jnp.float32)
    sigmoid_gate = jax.nn.sigmoid(gate_pre.astype(jnp.float32))
    mixer_float = mixer_out.astype(jnp.float32)
    gated_out = (mixer_float * sigmoid_gate).astype(jnp.bfloat16)
    weight_share = lax.psum_scatter(
        jnp.einsum("te,tc->ec", full_grad, gated_out, preferred_element_type=jnp.float32).astype(
            jnp.bfloat16
        ),
        "seq",
        scatter_dimension=0,
        tiled=True,
    )
    mixer_grad = (head_grad * sigmoid_gate).astype(jnp.bfloat16)
    gate_grad = (head_grad * mixer_float * sigmoid_gate * (1.0 - sigmoid_gate)).astype(jnp.bfloat16)
    grad_spread = to_offsets(
        mixer_grad.reshape(block_count, block_span, channels), seq_count, ch_count
    )
    offset_grad = jnp.einsum(
        "pcqkd,scikd->kpqsi", grad_spread, section_spread, preferred_element_type=jnp.float32
    ).reshape(offsets, total_blocks, total_blocks)
    section_grad_spread = jnp.einsum(
        "kpqsi,pcqkd->scikd", masked_two, grad_spread, preferred_element_type=jnp.float32
    ).astype(jnp.bfloat16)
    offset_grad = jnp.where(mask_two, offset_grad, jnp.zeros_like(offset_grad)).astype(jnp.bfloat16)
    section_grad = to_blocks(section_grad_spread, seq_count, ch_count)
    partial_grad = jnp.einsum(
        "ikd,ijd->ikj", section_grad, inputs, preferred_element_type=jnp.float32
    )
    partial_grad = jnp.where(mask_one, partial_grad, jnp.zeros_like(partial_grad))
    block_grad = lax.psum_scatter(
        partial_grad.astype(jnp.bfloat16), "ch", scatter_dimension=1, tiled=True
    )
    input_grad = jnp.einsum(
        "ikj,ikd->ijd", masked_one, section_grad, preferred_element_type=jnp.float32
    ).astype(jnp.bfloat16)
    return (
        input_grad.reshape(token_count, channels),
        gate_grad,
        block_grad,
        offset_grad,
        weight_share,
    )


def solution(mesh):
    in_specs = (
        P("seq", "ch"),
        P("seq", "ch"),
        P("seq", "ch"),
        P("seq", "ch", None),
        P(("seq", "ch"), None, None),
        P(None, "ch"),
        P(),
    )
    out_specs = (
        P("seq", "ch"),
        P("seq", "ch"),
        P("seq", "ch", None),
        P(("seq", "ch"), None, None),
        P("seq", "ch"),
    )
    return jax.shard_map(
        on_device, mesh=mesh, in_specs=in_specs, out_specs=out_specs, check_vma=False
    )
```

profile of v0, /device:TPU:6, one launch (start us, length us, event | category | flops | bytes accessed | tf_op | source)
XLA Modules:
  0.0 2105.8 jit_solution(565953672333166698)
XLA Ops:
  7.2 0.0 copy-start
  7.2 0.0 all-gather.3.cloned.1.call-start
  7.2 0.7 all-gather.3.cloned.1.call-update
  7.9 0.0 all-gather.5.cloned.1.call-start
  8.0 0.7 all-gather.5.cloned.1.call-update
  8.7 0.1 iota_compare_fusion
  8.9 0.0 copy-start.4
  8.9 106.9 %all-gather.3.cloned.1.call-done = bf16[32,512,512]{2,1,0:T(8,128)(2,1)} async-done(((bf16[32,128,512]{2,1,0:T(8,128)(2,1)}), bf16[32,512,512]{2,1,0:T(8,128)(2,1)}) %all-gather.3.cloned.1.call-update) | async-done | bytes 16777232 | tf_op jit(solution)/shard_map/all_gather | solution.py:57
  115.8 26.4 %convert_bitcast_fusion.1 = bf16[1,32,512,512]{3,2,1,0:T(8,128)(2,1)} fusion(bf16[32,512,512]{2,1,0:T(8,128)(2,1)} %bitcast.95, bf16[32,512,512]{2,1,0:T(8,128)(2,1)} %all-gather.3.cloned.1.call-done, pred[32,512]{1,0:T(8,128)(4,1)S(1)} %constant_dynamic-slice_fusion), kind=kOutput, calls=%fused_computation.23 | convolution fusion | flops 8615100416 | bytes 50348032 | tf_op jit(solution)/shard_map/ikj,ijd->ikd/dot_general | solution.py:68
  142.1 20.2 copy.82
  162.3 6.2 all-to-all-start.2
  168.6 0.3 reduce-window.9
  168.9 0.1 slice.7
  169.0 0.1 slice_reduce_fusion
  169.2 0.1 bitcast_subtract_fusion
  169.2 0.1 add_bitcast_fusion
  169.4 0.1 copy.75
  169.4 2.9 compare_select_fusion.9
  172.4 10.0 reshape.71
  182.4 364.9 %all-to-all-done.2 = bf16[1,32,512,512]{3,1,0,2:T(8,128)(2,1)} async-done(((bf16[1,32,512,512]{3,1,0,2:T(8,128)(2,1)}), bf16[1,32,512,512]{3,1,0,2:T(8,128)(2,1)}, u32[]{:S(2)}, u32[]{:S(2)}) %all-to-all-start.2) | async-done | bytes 16777248 | tf_op jit(solution)/shard_map/all_to_all | solution.py:20
  547.3 16.9 copy.83
  564.2 37.1 %fusion.6 = bf16[8,4,32,16,512]{4,2,0,1,3:T(8,128)(2,1)} fusion(bf16[8,4,32,16,512,1]{4,3,1,0,2,5:T(8,128)(2,1)} %bitcast.90, bf16[16,8,32,8,32,1]{4,3,2,1,0,5:T(8,128)(2,1)} %bitcast.88), kind=kOutput, calls=%fused_computation.15 | convolution fusion | flops 4303355904 | bytes 35651584 | tf_op jit(solution)/shard_map/kpqsi,scikd->pcqkd/dot_general | solution.py:76
  601.3 15.9 copy.87
  617.2 365.9 %all_to_all.54 = bf16[32,32,16,512]{3,2,1,0:T(8,128)(2,1)} all-to-all(bf16[32,32,16,512]{3,2,1,0:T(8,128)(2,1)S(1)} %bitcast.87), channel_id=1, replica_groups=mesh['seq'=8,'ch'=4] {'seq','ch'}, dimensions={0} | all-to-all | bytes 33554432 | tf_op jit(solution)/shard_map/all_to_all | solution.py:36
  983.2 9.9 convert_bitcast_fusion
  993.0 11.6 copy.88
  1004.6 63.6 %fusion.4 = (bf16[16384,512]{1,0:T(8,128)(2,1)}, bf16[16384,512]{1,0:T(8,128)(2,1)}, bf16[16384,512]{1,0:T(8,128)(2,1)}) fusion(f32[1,32,32,16,512]{4,3,2,1,0:T(8,128)} %copy.88, bf16[16384,512]{1,0:T(8,128)(2,1)} %param.8, bf16[16384,2048]{1,0:T(8,128)(2,1)} %all-gather.5.cloned.1.call-done, bf16[2048,512]{1,0:T(8,128)(2,1)S(1)} %copy-done), kind=kOutput, calls=%fused_computation.9 | convolution fusion | flops 34468790272 | bytes 169869312 | tf_op jit(solution)/shard_map/dot_general | solution.py:80
  1068.2 15.9 copy.72
  1084.1 367.1 %all_to_all.55 = bf16[1,32,512,512]{3,1,0,2:T(8,128)(2,1)S(1)} all-to-all(bf16[1,32,512,512]{3,1,0,2:T(8,128)(2,1)S(1)} %copy.72), channel_id=1, replica_groups=mesh['seq'=8,'ch'=4] {'seq','ch'}, dimensions={2} | all-to-all | bytes 33554432 | tf_op jit(solution)/shard_map/all_to_all | solution.py:20
  1451.2 20.5 copy.73
  1471.8 35.7 %fusion.5 = bf16[8,4,32,16,512]{4,2,0,1,3:T(8,128)(2,1)} fusion(bf16[8,4,32,16,512,1]{4,3,1,0,2,5:T(8,128)(2,1)} %bitcast.84, bf16[16,8,32,8,32,1]{4,3,2,1,0,5:T(8,128)(2,1)} %bitcast.89), kind=kOutput, calls=%fused_computation.14 | convolution fusion | flops 4303355904 | bytes 35651584 | tf_op jit(solution)/shard_map/kpqsi,pcqkd->scikd/dot_general | solution.py:100
  1507.4 18.5 copy.79
  1525.9 4.2 all-to-all-start.1
  1530.1 0.0 reduce-scatter.5.cloned.1.call-start
  1530.1 44.5 %fusion.31 = bf16[2048,512]{0,1:T(8,128)(2,1)} fusion(bf16[16384,512]{1,0:T(8,128)(2,1)} %get-tuple-element.30, bf16[16384,2048]{1,0:T(8,128)(2,1)} %all-gather.5.cloned.1.call-done), kind=kOutput, calls=%fused_computation.36 | convolution fusion | flops 34360786944 | bytes 85983232 | tf_op jit(solution)/shard_map/te,tc->ec/dot_general | solution.py:85
  1574.6 0.0 reduce-scatter.5.cloned.1.call-update
  1574.6 0.0 reduce-scatter.3.cloned.1.call-start
  1574.6 350.6 %all-to-all-done.1 = bf16[32,32,16,512]{3,2,1,0:T(8,128)(2,1)} async-done(((bf16[32,32,16,512]{3,2,1,0:T(8,128)(2,1)}), bf16[32,32,16,512]{3,2,1,0:T(8,128)(2,1)}, u32[]{:S(2)}, u32[]{:S(2)}) %all-to-all-start.1) | async-done | bytes 16777248 | tf_op jit(solution)/shard_map/all_to_all | solution.py:36
  1925.3 14.1 copy.80
  1939.4 21.5 %fusion = bf16[32,512,512]{2,1,0:T(8,128)(2,1)} fusion(pred[32,512]{1,0:T(8,128)(4,1)S(1)} %copy-done.5, bf16[32,512,512]{2,1,0:T(8,128)(2,1)} %bitcast.92, bf16[32,512,512]{2,1,0:T(8,128)(2,1)} %bitcast.96), kind=kOutput, calls=%fused_computation.2 | convolution fusion | flops 8615100416 | bytes 50348032 | tf_op jit(solution)/shard_map/ikd,ijd->ikj/dot_general | solution.py:105
  1960.9 0.0 reduce-scatter.3.cloned.1.call-update
  1960.9 0.0 reduce-scatter.5.cloned.1.call-done
  1961.0 1.8 copy.92
  1962.8 85.1 %fusion.21 = bf16[16,8,32,8,32]{4,2,3,1,0:T(8,128)(2,1)} fusion(bf16[8,4,32,16,512,1]{4,3,1,0,2,5:T(8,128)(2,1)} %bitcast.91, bf16[8,4,32,16,512,1]{4,3,1,0,2,5:T(8,128)(2,1)} %bitcast.85), kind=kOutput, calls=%fused_computation.27 | convolution fusion | flops 4294967296 | bytes 35651584 | tf_op jit(solution)/shard_map/pcqkd,scikd->kpqsi/dot_general | solution.py:97
  2047.9 15.5 copy.91
  2063.4 9.8 reshape.79
  2073.2 1.7 fusion.30
  2074.9 23.9 %fusion.16 = bf16[32,512,512]{2,1,0:T(8,128)(2,1)} fusion(bf16[32,512,512]{2,1,0:T(8,128)(2,1)} %bitcast.93, bf16[32,512,512]{2,1,0:T(8,128)(2,1)} %all-gather.3.cloned.1.call-done, pred[32,512]{1,0:T(8,128)(4,1)S(1)} %copy-done.5), kind=kOutput, calls=%fused_computation.26 | convolution fusion | flops 8615100416 | bytes 50348032 | tf_op jit(solution)/shard_map/ikj,ikd->ijd/dot_general | solution.py:112
  (17 shorter events, 0.1 us)
Async XLA Ops:
  7.2 997.5 %copy-start = (bf16[2048,512]{1,0:T(8,128)(2,1)S(1)}, bf16[2048,512]{1,0:T(8,128)(2,1)}, u32[]{:S(2)}) copy-start(bf16[2048,512]{1,0:T(8,128)(2,1)} %param.12) | copy-start | bytes 6291460
  7.2 1.5 copy-start.6
  7.2 108.6 %all-gather.3.cloned.1.call-start = ((), (), s32[]{:S(2)}) async-start(), calls=%async_computation.6 | async-start | bytes 20971520 | tf_op jit(solution)/shard_map/all_gather | solution.py:57
  7.9 996.7 %all-gather.5.cloned.1.call-start = ((), (), s32[]{:S(2)}) async-start(), calls=%async_computation.7 | async-start | bytes 83886080 | tf_op jit(solution)/shard_map/all_gather | solution.py:56
  8.9 133.3 %copy-start.4 = (pred[32,512]{1,0:T(8,128)(4,1)}, pred[32,512]{1,0:T(8,128)(4,1)S(1)}, u32[]{:S(2)}) copy-start(pred[32,512]{1,0:T(8,128)(4,1)S(1)} %constant_dynamic-slice_fusion) | copy-start | bytes 49156
  162.3 385.0 %all-to-all-start.2 = ((bf16[1,32,512,512]{3,1,0,2:T(8,128)(2,1)}), bf16[1,32,512,512]{3,1,0,2:T(8,128)(2,1)}, u32[]{:S(2)}, u32[]{:S(2)}) async-start(bf16[1,32,512,512]{3,1,0,2:T(8,128)(2,1)} %copy.82), calls=%async_computation.2 | async-start | bytes 33554432 | tf_op jit(solution)/shard_map/all_to_all | solution.py:20
  169.4 394.8 %copy-start.2 = (s32[16,256]{1,0:T(8,128)}, s32[16,256]{1,0:T(8,128)S(1)}, u32[]{:S(2)}) copy-start(s32[16,256]{1,0:T(8,128)S(1)} %copy.75) | copy-start | bytes 49156
  1525.9 399.4 %all-to-all-start.1 = ((bf16[32,32,16,512]{3,2,1,0:T(8,128)(2,1)}), bf16[32,32,16,512]{3,2,1,0:T(8,128)(2,1)}, u32[]{:S(2)}, u32[]{:S(2)}) async-start(bf16[32,32,16,512]{3,2,1,0:T(8,128)(2,1)} %bitcast.86), calls=%async_computation.1 | async-start | bytes 33554432 | tf_op jit(solution)/shard_map/all_to_all | solution.py:36
  1530.1 430.9 %reduce-scatter.5.cloned.1.call-start = ((), (), s32[]{:S(2)}) async-start(), calls=%async_computation.9 | async-start | bytes 2359296 | tf_op jit(solution)/shard_map/reduce_scatter | solution.py:84
  1574.6 524.2 %reduce-scatter.3.cloned.1.call-start = ((), (), s32[]{:S(2)}) async-start(), calls=%async_computation.8 | async-start | bytes 20971520 | tf_op jit(solution)/shard_map/reduce_scatter | solution.py:109
  1925.3 14.1 copy-start.5
  2047.9 25.3 %copy-start.3 = (s32[16,256]{1,0:T(8,128)S(1)}, s32[16,256]{1,0:T(8,128)}, u32[]{:S(2)}) copy-start(s32[16,256]{1,0:T(8,128)} %copy-done.2) | copy-start | bytes 49156
  2074.9 23.9 %copy-start.1 = (bf16[2048,512]{1,0:T(8,128)(2,1)S(1)}, bf16[2048,512]{1,0:T(8,128)(2,1)}, u32[]{:S(2)}) copy-start(bf16[2048,512]{1,0:T(8,128)(2,1)} %param.12) | copy-start | bytes 6291460
Sparse Core Ops, SparseCore 0:
  9.6 106.1 all-gather.2
  117.3 712.8 all-gather.4
  1574.7 177.2 reduce-scatter.4
  1961.1 122.2 reduce-scatter.2
where the time goes:
time: 2110 us
  waiting for transfers between devices  824 us (39%)
  blocking collectives  733 us (35%)
  matrix products  338 us (16%)
  local copies, waits for them, and re-layouts  171 us (8%)
    all_to_all x1, blocking collectives, to_offsets(): lax.all_to_all(blocked.reshape(1, block_count, block_span, channels), ('s...  367 us
    all_to_all x1, blocking collectives, to_blocks(): lax.all_to_all(spread.reshape(seq_count * ch_count, block_count, offsets,...  366 us
    all_to_all x1, waiting for transfers between devices, to_offsets(): lax.all_to_all(blocked.reshape(1, block_count, block_span, channels), ('s...  365 us
    all_to_all x1, waiting for transfers between devices, to_blocks(): lax.all_to_all(spread.reshape(seq_count * ch_count, block_count, offsets,...  351 us
    all_gather x1, waiting for transfers between devices, on_device(): lax.all_gather(block_weight, 'ch', axis=1, tiled=True)  107 us
    dot_general x1, matrix products, on_device(): jnp.einsum('pcqkd,scikd->kpqsi', grad_spread, section_spread, preferred_e...  85.1 us
    dot_general x1, matrix products, on_device(): jnp.dot(full_grad, out_weight, preferred_element_type=jnp.float32)  63.6 us
    dot_general x1, matrix products, on_device(): jnp.einsum('te,tc->ec', full_grad, gated_out, preferred_element_type=jnp....  44.5 us
  transfers between devices with their start and end apart: 6, of which 3 were waited for; matrix products, arithmetic and copies ran while one was open for 18% of the time, Pallas kernels for 0%

commit v1 on v0

--- a/solution.py
+++ b/solution.py
@@ -2,6 +2,15 @@
 import jax.numpy as jnp
 from jax import lax
 from jax.sharding import PartitionSpec as P
+from jax.lax import all_to_all, axis_size
+
+
+def apply_samples(obj, chip_axis, ndim_at, where_dim):
+    part_now = jnp.split(obj, axis_size(chip_axis), ndim_at)
+    reached = jnp.stack(part_now, 0)
+    all_rows = all_to_all(reached, axis_name=chip_axis, split_axis=0, concat_axis=0)
+    taken_in = jnp.concatenate(all_rows, where_dim)
+    return taken_in
 
 
 def side_flags_of(reset_offset, block_span):
@@ -33,12 +42,8 @@
     block_count = spread.shape[2]
     offsets = spread.shape[3]
     channels = spread.shape[4]
-    arrived = lax.all_to_all(
-        spread.reshape(seq_count * ch_count, block_count, offsets, channels),
-        ("seq", "ch"),
-        split_axis=0,
-        concat_axis=2,
-        tiled=True,
+    arrived = apply_samples(
+        spread.reshape(seq_count * ch_count, block_count, offsets, channels), ("seq", "ch"), 0, 2
     )
     return arrived.reshape(block_count, offsets * seq_count * ch_count, channels)
 

time: 2110 us -> 2140 us (1.014)
  local copies, waits for them, and re-layouts: 171 us -> 196 us
    unnamed x15 -> x77, local copies, waits for them, and re-layouts: 1.83 us -> 28.9 us
  transfers between devices with their start and end apart: 6 -> 6, of which waited for: 3 -> 3; matrix products, arithmetic and copies ran while one was open for 18% -> 17% of each run, Pallas kernels for 0% -> 0%
where the time goes in v1:
time: 2140 us; the launch traced here: 2130 us
  waiting for transfers between devices  825 us (39%)
  blocking collectives  733 us (34%)
  matrix products  337 us (16%)
  local copies, waits for them, and re-layouts  196 us (9%)
    all_to_all x1, blocking collectives, to_offsets(): lax.all_to_all(blocked.reshape(1, block_count, block_span, channels), ('s...  367 us
    all_to_all x1, blocking collectives, apply_samples(): all_to_all(reached, axis_name=chip_axis, split_axis=0, concat_axis=0)  366 us
    all_to_all x1, waiting for transfers between devices, to_offsets(): lax.all_to_all(blocked.reshape(1, block_count, block_span, channels), ('s...  365 us
    all_to_all x1, waiting for transfers between devices, apply_samples(): all_to_all(reached, axis_name=chip_axis, split_axis=0, concat_axis=0)  352 us
    all_gather x1, waiting for transfers between devices, on_device(): lax.all_gather(block_weight, 'ch', axis=1, tiled=True)  107 us
    dot_general x1, matrix products, on_device(): jnp.einsum('pcqkd,scikd->kpqsi', grad_spread, section_spread, preferred_e...  85.1 us
    dot_general x1, matrix products, on_device(): jnp.dot(full_grad, out_weight, preferred_element_type=jnp.float32)  63.6 us
    dot_general x1, matrix products, on_device(): jnp.einsum('te,tc->ec', full_grad, gated_out, preferred_element_type=jnp....  44.1 us
  transfers between devices with their start and end apart: 6, of which 3 were waited for; matrix products, arithmetic and copies ran while one was open for 17% of the time, Pallas kernels for 0%

profile of v1, /device:TPU:6, one launch (start us, length us, event | category | flops | bytes accessed | tf_op | source)
XLA Modules:
  0.0 2132.2 jit_solution(4094296755905292350)
XLA Ops:
  8.9 106.9 %all-gather.3.cloned.1.call-done = bf16[32,512,512]{2,1,0:T(8,128)(2,1)} async-done(((bf16[32,128,512]{2,1,0:T(8,128)(2,1)}), bf16[32,512,512]{2,1,0:T(8,128)(2,1)}) %all-gather.3.cloned.1.call-update) | async-done | bytes 16777232 | tf_op jit(solution)/shard_map/all_gather | solution.py:62
  115.8 26.4 %convert_bitcast_fusion.1 = bf16[1,32,512,512]{3,2,1,0:T(8,128)(2,1)} fusion(bf16[32,512,512]{2,1,0:T(8,128)(2,1)} %bitcast.408, bf16[32,512,512]{2,1,0:T(8,128)(2,1)} %all-gather.3.cloned.1.call-done, pred[32,512]{1,0:T(8,128)(4,1)S(1)} %constant_dynamic-slice_fusion), kind=kOutput, calls=%fused_computation.23 | convolution fusion | flops 8615100416 | bytes 50348032 | tf_op jit(solution)/shard_map/ikj,ijd->ikd/dot_general | solution.py:73
  142.1 20.2 copy.144
  162.3 6.2 all-to-all-start.2
  169.4 2.9 compare_select_fusion.9
  172.4 10.0 reshape.68
  182.4 364.9 %all-to-all-done.2 = bf16[1,32,512,512]{3,1,0,2:T(8,128)(2,1)} async-done(((bf16[1,32,512,512]{3,1,0,2:T(8,128)(2,1)}), bf16[1,32,512,512]{3,1,0,2:T(8,128)(2,1)}, u32[]{:S(2)}, u32[]{:S(2)}) %all-to-all-start.2) | async-done | bytes 16777248 | tf_op jit(solution)/shard_map/all_to_all | solution.py:29
  547.3 16.9 copy.145
  564.2 37.1 %fusion.6 = bf16[8,4,32,16,512]{4,2,0,1,3:T(8,128)(2,1)} fusion(bf16[8,4,32,16,512,1]{4,3,1,0,2,5:T(8,128)(2,1)} %bitcast.403, bf16[16,8,32,8,32,1]{4,3,2,1,0,5:T(8,128)(2,1)} %bitcast.401), kind=kOutput, calls=%fused_computation.15 | convolution fusion | flops 4303355904 | bytes 35651584 | tf_op jit(solution)/shard_map/kpqsi,scikd->pcqkd/dot_general | solution.py:81
  601.3 15.9 copy.149
  618.6 365.9 %all_to_all.40 = bf16[32,1,32,16,512]{4,3,2,1,0:T(8,128)(2,1)} all-to-all(bf16[32,1,32,16,512]{4,3,2,1,0:T(8,128)(2,1)S(1)} %fusion.32), channel_id=1, replica_groups=mesh['seq'=8,'ch'=4] {'seq','ch'}, dimensions={0} | all-to-all | bytes 33554432 | tf_op jit(solution)/shard_map/all_to_all | solution.py:11
  984.6 9.9 convert_bitcast_fusion
  994.4 11.6 copy.150
  1006.1 63.6 %fusion.4 = (bf16[16384,512]{1,0:T(8,128)(2,1)}, bf16[16384,512]{1,0:T(8,128)(2,1)}, bf16[16384,512]{1,0:T(8,128)(2,1)}) fusion(f32[1,32,32,16,512]{4,3,2,1,0:T(8,128)} %copy.150, bf16[16384,512]{1,0:T(8,128)(2,1)} %param.8, bf16[16384,2048]{1,0:T(8,128)(2,1)} %all-gather.5.cloned.1.call-done, bf16[2048,512]{1,0:T(8,128)(2,1)S(1)} %copy-done), kind=kOutput, calls=%fused_computation.8 | convolution fusion | flops 34468790272 | bytes 169869312 | tf_op jit(solution)/shard_map/dot_general | solution.py:85
  1069.6 15.9 copy.134
  1085.5 367.1 %all_to_all.41 = bf16[1,32,512,512]{3,1,0,2:T(8,128)(2,1)S(1)} all-to-all(bf16[1,32,512,512]{3,1,0,2:T(8,128)(2,1)S(1)} %copy.134), channel_id=1, replica_groups=mesh['seq'=8,'ch'=4] {'seq','ch'}, dimensions={2} | all-to-all | bytes 33554432 | tf_op jit(solution)/shard_map/all_to_all | solution.py:29
  1452.6 20.5 copy.135
  1473.2 35.7 %fusion.5 = bf16[8,4,32,16,512]{4,2,0,1,3:T(8,128)(2,1)} fusion(bf16[8,4,32,16,512,1]{4,3,1,0,2,5:T(8,128)(2,1)} %bitcast.399, bf16[16,8,32,8,32,1]{4,3,2,1,0,5:T(8,128)(2,1)} %bitcast.402), kind=kOutput, calls=%fused_computation.14 | convolution fusion | flops 4303355904 | bytes 35651584 | tf_op jit(solution)/shard_map/kpqsi,pcqkd->scikd/dot_general | solution.py:105
  1508.9 15.9 copy.141
  1524.8 0.8 fusion.95
  1525.7 0.8 fusion.94
  1526.5 0.9 fusion.93
  1528.2 0.9 fusion.91
  1529.0 0.8 fusion.90
  1531.5 0.8 fusion.87
  1533.2 0.9 fusion.85
  1535.7 0.8 fusion.82
  1537.3 0.9 fusion.80
  1538.2 0.9 fusion.79
  1539.1 0.8 fusion.78
  1539.9 0.8 fusion.77
  1543.2 0.8 fusion.73
  1544.0 0.8 fusion.72
  1544.9 0.9 fusion.71
  1545.8 0.9 fusion.70
  1548.3 0.8 fusion.67
  1550.8 0.9 fusion.64
  1551.6 4.2 all-to-all-start.1
  1555.8 44.1 %fusion.31 = bf16[2048,512]{0,1:T(8,128)(2,1)} fusion(bf16[16384,512]{1,0:T(8,128)(2,1)} %get-tuple-element.30, bf16[16384,2048]{1,0:T(8,128)(2,1)} %all-gather.5.cloned.1.call-done), kind=kOutput, calls=%fused_computation.36 | convolution fusion | flops 34360786944 | bytes 85983232 | tf_op jit(solution)/shard_map/te,tc->ec/dot_general | solution.py:90
  1600.0 351.7 %all-to-all-done.1 = bf16[32,1,32,16,512]{4,3,2,1,0:T(8,128)(2,1)} async-done(((bf16[32,1,32,16,512]{4,3,2,1,0:T(8,128)(2,1)}), bf16[32,1,32,16,512]{4,3,2,1,0:T(8,128)(2,1)}, u32[]{:S(2)}, u32[]{:S(2)}) %all-to-all-start.1) | async-done | bytes 16777248 | tf_op jit(solution)/shard_map/all_to_all | solution.py:11
  1951.7 14.1 copy.142
  1965.8 21.5 %fusion = bf16[32,512,512]{2,1,0:T(8,128)(2,1)} fusion(pred[32,512]{1,0:T(8,128)(4,1)S(1)} %copy-done.5, bf16[32,512,512]{2,1,0:T(8,128)(2,1)} %bitcast.405, bf16[32,512,512]{2,1,0:T(8,128)(2,1)} %bitcast.409), kind=kOutput, calls=%fused_computation.2 | convolution fusion | flops 8615100416 | bytes 50348032 | tf_op jit(solution)/shard_map/ikd,ijd->ikj/dot_general | solution.py:110
  1987.3 1.8 copy.154
  1989.1 85.1 %fusion.21 = bf16[16,8,32,8,32]{4,2,3,1,0:T(8,128)(2,1)} fusion(bf16[8,4,32,16,512,1]{4,3,1,0,2,5:T(8,128)(2,1)} %bitcast.404, bf16[8,4,32,16,512,1]{4,3,1,0,2,5:T(8,128)(2,1)} %bitcast.400), kind=kOutput, calls=%fused_computation.27 | convolution fusion | flops 4294967296 | bytes 35651584 | tf_op jit(solution)/shard_map/pcqkd,scikd->kpqsi/dot_general | solution.py:102
  2074.3 15.5 copy.153
  2089.8 9.8 reshape.76
  2099.6 1.7 fusion.30
  2101.3 23.9 %fusion.16 = bf16[32,512,512]{2,1,0:T(8,128)(2,1)} fusion(bf16[32,512,512]{2,1,0:T(8,128)(2,1)} %bitcast.406, bf16[32,512,512]{2,1,0:T(8,128)(2,1)} %all-gather.3.cloned.1.call-done, pred[32,512]{1,0:T(8,128)(4,1)S(1)} %copy-done.5), kind=kOutput, calls=%fused_computation.26 | convolution fusion | flops 8615100416 | bytes 50348032 | tf_op jit(solution)/shard_map/ikj,ikd->ijd/dot_general | solution.py:117
  (81 shorter events, 15.3 us)
Async XLA Ops:
  7.2 998.9 %copy-start = (bf16[2048,512]{1,0:T(8,128)(2,1)S(1)}, bf16[2048,512]{1,0:T(8,128)(2,1)}, u32[]{:S(2)}) copy-start(bf16[2048,512]{1,0:T(8,128)(2,1)} %param.12) | copy-start | bytes 6291460
  7.2 1.5 copy-start.6
  7.2 108.6 %all-gather.3.cloned.1.call-start = ((), (), s32[]{:S(2)}) async-start(), calls=%async_computation.6 | async-start | bytes 20971520 | tf_op jit(solution)/shard_map/all_gather | solution.py:62
  7.9 998.1 %all-gather.5.cloned.1.call-start = ((), (), s32[]{:S(2)}) async-start(), calls=%async_computation.7 | async-start | bytes 83886080 | tf_op jit(solution)/shard_map/all_gather | solution.py:61
  8.9 133.3 %copy-start.4 = (pred[32,512]{1,0:T(8,128)(4,1)}, pred[32,512]{1,0:T(8,128)(4,1)S(1)}, u32[]{:S(2)}) copy-start(pred[32,512]{1,0:T(8,128)(4,1)S(1)} %constant_dynamic-slice_fusion) | copy-start | bytes 49156
  162.3 385.0 %all-to-all-start.2 = ((bf16[1,32,512,512]{3,1,0,2:T(8,128)(2,1)}), bf16[1,32,512,512]{3,1,0,2:T(8,128)(2,1)}, u32[]{:S(2)}, u32[]{:S(2)}) async-start(bf16[1,32,512,512]{3,1,0,2:T(8,128)(2,1)} %copy.144), calls=%async_computation.2 | async-start | bytes 33554432 | tf_op jit(solution)/shard_map/all_to_all | solution.py:29
  169.4 394.8 %copy-start.2 = (s32[16,256]{1,0:T(8,128)}, s32[16,256]{1,0:T(8,128)S(1)}, u32[]{:S(2)}) copy-start(s32[16,256]{1,0:T(8,128)S(1)} %copy.137) | copy-start | bytes 49156
  1551.6 400.0 %all-to-all-start.1 = ((bf16[32,1,32,16,512]{4,3,2,1,0:T(8,128)(2,1)}), bf16[32,1,32,16,512]{4,3,2,1,0:T(8,128)(2,1)}, u32[]{:S(2)}, u32[]{:S(2)}) async-start(bf16[32,1,32,16,512]{4,3,2,1,0:T(8,128)(2,1)} %fusion.64), calls=%async_computation.1 | async-start | bytes 33554432 | tf_op jit(solution)/shard_map/all_to_all | solution.py:11
  1555.8 431.6 %reduce-scatter.5.cloned.1.call-start = ((), (), s32[]{:S(2)}) async-start(), calls=%async_computation.9 | async-start | bytes 2359296 | tf_op jit(solution)/shard_map/reduce_scatter | solution.py:89
  1599.9 525.3 %reduce-scatter.3.cloned.1.call-start = ((), (), s32[]{:S(2)}) async-start(), calls=%async_computation.8 | async-start | bytes 20971520 | tf_op jit(solution)/shard_map/reduce_scatter | solution.py:114
  1951.7 14.1 copy-start.5
  2074.3 25.3 %copy-start.3 = (s32[16,256]{1,0:T(8,128)S(1)}, s32[16,256]{1,0:T(8,128)}, u32[]{:S(2)}) copy-start(s32[16,256]{1,0:T(8,128)} %copy-done.2) | copy-start | bytes 49156
  2101.3 23.9 %copy-start.1 = (bf16[2048,512]{1,0:T(8,128)(2,1)S(1)}, bf16[2048,512]{1,0:T(8,128)(2,1)}, u32[]{:S(2)}) copy-start(bf16[2048,512]{1,0:T(8,128)(2,1)} %param.12) | copy-start | bytes 6291460
Sparse Core Ops, SparseCore 0:
  9.6 106.1 all-gather.2
  117.3 712.8 all-gather.4
  1600.0 177.9 reduce-scatter.4
  1987.4 122.2 reduce-scatter.2
